TPU v7x, 32 devices: a whole 2x2x4 slice. The times are simulated.
32 devices in a mesh: hour: 16 (over z, y, x), region: 2 (over core).
Axes of the slice: x: 2, y: 2, z: 4, core: 2. Of those that a mesh axis runs over, the one named last changes fastest.
Arguments:
- demand: float32 [2240, 1024], P('hour', 'region'), may hold values from 0.2 to 2
- avail_factor: bfloat16 [2240, 8, 1024], P('hour', None, 'region'), may hold values from 0 to 1
- tech_mask: int32 [8, 1024], P(None, 'region'), may hold values 0 or 1
- var_cost: float32 [8, 1024], P(None, 'region'), may hold values from 0.1 to 2
- inv_cost: float32 [8, 1024], P(None, 'region'), may hold values from 0.2 to 1
- ramp_rate: float32 [8, 1024], P(None, 'region'), may hold values from 0.1 to 1
- network: float32 [1024, 1024], P('region'), as said below
- pattern: int32 [8, 8], replicated, may hold values from 0 to 1, as said below
- live_hours: int32 [1], replicated, may hold values from 1961 to 2100
- generation: float32 [2240, 8, 1024], P('hour', None, 'region'), may hold values from 0 to 1
- angles: float32 [2240, 1024], P('hour', 'region'), may hold values from -3 to 3
- levels: float32 [2240, 1024], P('hour', 'region'), may hold values from 0 to 2
- net_power: float32 [2240, 1024], P('hour', 'region'), may hold values from -3 to 3
- capacity: float32 [8, 1024], P(None, 'region'), may hold values from 0.5 to 2
- balance_dual: float32 [2240, 1024], P('hour', 'region'), may hold values from -3 to 3
- storage_dual: float32 [2240, 1024], P('hour', 'region'), may hold values from -3 to 3
- limit_dual: float32 [2240, 8, 1024], P('hour', None, 'region'), may hold values from 0 to 1.5
- ramp_dual: float32 [2240, 8, 1024], P('hour', None, 'region'), may hold values from 0 to 0.5
Outputs:
- final_generation: float32 [2240, 8, 1024], P('hour', None, 'region')
- final_angles: float32 [2240, 1024], P('hour', 'region')
- final_levels: float32 [2240, 1024], P('hour', 'region')
- final_power: float32 [2240, 1024], P('hour', 'region')
- final_capacity: float32 [8, 1024], P(None, 'region')
- final_balance: float32 [2240, 1024], P('hour', 'region')
- final_storage: float32 [2240, 1024], P('hour', 'region')
- final_limit: float32 [2240, 8, 1024], P('hour', None, 'region')
- final_ramp: float32 [2240, 8, 1024], P('hour', None, 'region')
Inputs may be any that keep to these rules, and one draw needn't show every extreme that they name: pattern is symmetric with ones on its diagonal. network is symmetric.
All inputs are finite; a program needn't handle non-finite values. No bound on the sum of `tech_mask` on one device may be relied on, other than what follows from the above.
Results may differ from a plain program's by a relative error of at most 0.0003.
Values sent between devices are 32-bit elements; how exact they have to be, the bound alone decides.
No kernel may reach another device: no remote copies, remote signals or barrier semaphores. Data moves between devices by JAX's collectives and lax.ppermute only.
A program may use at most 64 MiB of HBM per device.

v0:
```python
import jax
import jax.numpy as jnp
from jax import lax
from jax.sharding import PartitionSpec as P

BUS = 1024
TECH = 8
BLOCK = 128
ITERS = 2
primal_step = 0.2
capacity_step = 4.0
dual_scale = 0.06


def shifted(block, axis, distance):
    devices = range(lax.axis_size(axis))
    route = [((i - distance) % len(devices), i) for i in devices]
    return lax.ppermute(block, axis, route)


def per_device(
    demand,
    avail_factor,
    tech_mask,
    var_cost,
    inv_cost,
    ramp_rate,
    network,
    pattern,
    live_hours,
    generation,
    angles,
    levels,
    net_power,
    capacity,
    balance_dual,
    storage_dual,
    limit_dual,
    ramp_dual,
):
    hour_rows = demand.shape[0]
    local_bus = demand.shape[1]
    total_hours = hour_rows * lax.axis_size("hour")
    first_hour = lax.axis_index("hour") * hour_rows
    live_rows = (first_hour + jnp.arange(hour_rows, dtype=jnp.int32) < live_hours[0]).astype(
        jnp.float32
    )
    available = (
        avail_factor.astype(jnp.float32)
        * tech_mask.astype(jnp.float32)[None]
        * live_rows[:, None, None]
    )
    live_load = demand * live_rows[:, None]
    blocks_here = local_bus // BLOCK
    pattern_rows = lax.dynamic_slice_in_dim(
        pattern, lax.axis_index("region") * blocks_here, blocks_here, 0
    )
    block_mask = jnp.repeat(jnp.repeat(pattern_rows.astype(jnp.float32), BLOCK, 0), BLOCK, 1)
    matrix = network * block_mask
    entry_count = float(total_hours * (TECH + 3) * BUS)

    def fold_part(segment):
        return lax.dot_general(
            segment,
            matrix,
            (((1,), (1,)), ((), ())),
            precision=lax.Precision.HIGHEST,
            preferred_element_type=jnp.float32,
        )

    for iteration in range(ITERS):
        behind = shifted((ramp_dual[-1:], storage_dual[-1:]), "hour", 1)
        prev_ramp = jnp.concatenate([behind[0], ramp_dual[:-1]], axis=0)
        prev_store = jnp.concatenate([behind[1], storage_dual[:-1]], axis=0)
        gen_new = jnp.maximum(
            0.0,
            generation
            - primal_step
            * (var_cost[None] + balance_dual[:, None, :] + limit_dual + prev_ramp - ramp_dual),
        )
        ang_new = angles + primal_step * fold_part(
            lax.all_gather(balance_dual, "region", axis=1, tiled=True)
        )
        pow_new = net_power - primal_step * (balance_dual + storage_dual)
        lev_new = jnp.maximum(0.0, levels - primal_step * (prev_store - storage_dual))
        square_part = (
            jnp.sum((gen_new - generation) ** 2)
            + jnp.sum((ang_new - angles) ** 2)
            + jnp.sum((pow_new - net_power) ** 2)
            + jnp.sum((lev_new - levels) ** 2)
        )
        invest_part = jnp.sum(available * limit_dual + ramp_rate[None] * ramp_dual, axis=0)
        invest = lax.psum(invest_part, "hour")
        squares = lax.psum(square_part, ("hour", "region"))
        cap_new = jnp.maximum(
            0.0, capacity - capacity_step * (inv_cost - invest / float(total_hours))
        )
        step_size = jnp.sqrt(squares / entry_count + 1e-06)
        dual_step = dual_scale / step_size
        gen_bar = 2.0 * gen_new - generation
        ang_bar = 2.0 * ang_new - angles
        pow_bar = 2.0 * pow_new - net_power
        lev_bar = 2.0 * lev_new - levels
        cap_bar = 2.0 * cap_new - capacity
        forward = shifted((gen_bar[:1], lev_bar[:1]), "hour", -1)
        next_gen = jnp.concatenate([gen_bar[1:], forward[0]], axis=0)
        next_level = jnp.concatenate([lev_bar[1:], forward[1]], axis=0)
        balance_dual = balance_dual + dual_step * (
            jnp.sum(gen_bar, axis=1)
            + pow_bar
            - fold_part(lax.all_gather(ang_bar, "region", axis=1, tiled=True))
            - live_load
        )
        storage_dual = storage_dual + dual_step * (next_level - lev_bar + pow_bar)
        limit_dual = jnp.maximum(
            0.0, limit_dual + dual_step * (gen_bar - available * cap_bar[None])
        )
        ramp_dual = jnp.maximum(
            0.0, ramp_dual + dual_step * (next_gen - gen_bar - ramp_rate[None] * cap_bar[None])
        )
        generation, angles, net_power, levels, capacity = (
            gen_new,
            ang_new,
            pow_new,
            lev_new,
            cap_new,
        )
    return (
        generation,
        angles,
        levels,
        net_power,
        capacity,
        balance_dual,
        storage_dual,
        limit_dual,
        ramp_dual,
    )


def solution(mesh):
    return jax.shard_map(
        per_device,
        mesh=mesh,
        in_specs=(
            P("hour", "region"),
            P("hour", None, "region"),
            P(None, "region"),
            P(None, "region"),
            P(None, "region"),
            P(None, "region"),
            P("region", None),
            P(),
            P(),
            P("hour", None, "region"),
            P("hour", "region"),
            P("hour", "region"),
            P("hour", "region"),
            P(None, "region"),
            P("hour", "region"),
            P("hour", "region"),
            P("hour", None, "region"),
            P("hour", None, "region"),
        ),
        out_specs=(
            P("hour", None, "region"),
            P("hour", "region"),
            P("hour", "region"),
            P("hour", "region"),
            P(None, "region"),
            P("hour", "region"),
            P("hour", "region"),
            P("hour", None, "region"),
            P("hour", None, "region"),
        ),
        check_vma=False,
    )
```

profile of v0, /device:TPU:0, one launch (start us, length us, event | category | flops | bytes accessed | tf_op | source)
XLA Modules:
  0.0 319.3 jit_solution(14245832103954252068)
XLA Ops:
  1.4 2.9 collective-permute-start.1
  5.0 1.5 collective-permute-start
  7.2 2.4 all_gather.12
  9.6 0.8 dynamic-slice_convert_fusion
  12.2 3.7 %multiply_subtract_fusion.7 = (f32[140,512]{1,0:T(8,128)S(1)}, f32[]{:T(128)}, f32[140,512]{1,0:T(8,128)}) fusion(f32[140,512]{1,0:T(8,128)S(1)} %copy-done.28, f32[512,1024]{1,0:T(8,128)S(1)} %bitcast_multiply_fusion, f32[140,1024]{1,0:T(8,128)S(1)} %all_gather.12), kind=kOutput, calls=%fused_computation.61 | convolution fusion | flops 881305600 | bytes 3530756 | tf_op jit(solution)/shard_map/dot_general | solution.py:63
  15.9 2.2 all_gather.13
  18.1 3.0 fusion.39
  22.3 3.0 multiply_subtract_fusion.6
  26.1 4.1 %collective-permute-start.4 = (f32[1,512]{1,0:T(1,128)S(1)}, f32[1,512]{1,0:T(1,128)S(1)}, u32[]{:S(2)}, u32[]{:S(2)}) collective-permute-start(f32[1,512]{1,0:T(1,128)S(1)} %slice.69), channel_id=1, source_target_pairs={{2,0},{4,2},{6,4},{8,6},{10,8},{12,10},{14,12},{16,14},{18,16},{20... | collective-permute-start | bytes 6152 | tf_op jit(solution)/shard_map/ppermute | solution.py:18
  30.2 6.1 %fusion.36 = (f32[140,512]{1,0:T(8,128)}, f32[140,8,512]{2,1,0:T(8,128)}, f32[140,8,512]{2,1,0:T(8,128)S(1)}, f32[8,512]{1,0:T(8,128)S(1)}) fusion(f32[140,8,512]{2,1,0:T(8,128)} %param.27, f32[140,8,512]{2,1,0:T(8,128)S(1)} %copy-done.5, f32[139,8,512]{2,1,0:T(8,128)S(1)} %slice-done, f32[1,8,512]{2,1,0:T(8,128)S(1)} %collective-permute-done, ...), kind=kLoop, calls=%fused_computation.74 | loop fusion | flops 10246144 | bytes 15548976 | tf_op jit(solution)/shard_map/reduce_sum | solution.py:109
  36.3 1.3 multiply_reduce_fusion.1
  40.2 1.7 slice.68
  41.9 37.6 %psum.28 = f32[]{:T(128)} all-reduce(f32[]{:T(128)S(6)} %add.149), channel_id=1, replica_groups=mesh['hour'=16,'region'=2] {'hour','region'}, use_global_device_ids=true, to_apply=%region_4.0 | all-reduce | flops 1 | bytes 8 | tf_op jit(solution)/shard_map/psum | solution.py:94
  80.3 3.3 %multiply_reduce_fusion.3 = (f32[]{:T(128)}, f32[140,512]{1,0:T(8,128)}, f32[140,512]{1,0:T(8,128)S(1)}, f32[140,512]{1,0:T(8,128)}) fusion(f32[140,512]{1,0:T(8,128)} %get-tuple-element.42, f32[140,512]{1,0:T(8,128)} %param.33, f32[140,512]{1,0:T(8,128)} %param.30, f32[140,512]{1,0:T(8,128)} %copy-done.20, f32[1,512]{1,0:T(1,128)S(1)} %collective-permute-done.4, ...), kind=kLoop, calls=%fused_computation.56 | loop fusion | flops 1361919 | bytes 3441208 | tf_op jit(solution)/shard_map/reduce_sum | solution.py:89
  84.3 2.3 collective-permute-start.5
  86.6 75.0 %psum.29 = f32[8,512]{1,0:T(8,128)S(1)} all-reduce(f32[8,512]{1,0:T(8,128)S(1)} %get-tuple-element.32), channel_id=1, replica_groups=mesh['hour'=16,'region'=2] {'hour'}, use_global_device_ids=true, to_apply=%region_7.0 | all-reduce | flops 4096 | bytes 32768 | tf_op jit(solution)/shard_map/psum | solution.py:93
  161.5 0.9 slice.65
  162.4 2.6 all_gather.14
  165.0 4.8 %multiply_reduce_fusion.4 = (f32[]{:T(128)}, f32[140,512]{1,0:T(8,128)}, f32[140,512]{1,0:T(8,128)}) fusion(f32[140,512]{1,0:T(8,128)} %get-tuple-element.43, f32[140,1024]{1,0:T(8,128)S(1)} %all_gather.14, f32[512,1024]{1,0:T(8,128)S(1)} %bitcast_multiply_fusion), kind=kOutput, calls=%fused_computation.57 | convolution fusion | flops 881305600 | bytes 3530756 | tf_op jit(solution)/shard_map/dot_general | solution.py:63
  171.7 0.9 fusion.7
  172.6 2.1 collective-permute-start.3
  175.5 4.4 %collective-permute-done.3 = f32[1,8,512]{2,1,0:T(8,128)S(1)} collective-permute-done((f32[1,8,512]{2,1,0:T(8,128)S(1)}, f32[1,8,512]{2,1,0:T(8,128)S(1)}, u32[]{:S(2)}, u32[]{:S(2)}) %collective-permute-start.3) | collective-permute-done | bytes 16416 | tf_op jit(solution)/shard_map/ppermute | solution.py:18
  180.0 4.3 %multiply_reduce_fusion = (f32[]{:T(128)}, f32[140,8,512]{2,1,0:T(8,128)}, f32[140,8,512]{2,1,0:T(8,128)}) fusion(f32[140,8,512]{2,1,0:T(8,128)S(1)} %copy-done.3, f32[140,8,512]{2,1,0:T(8,128)S(1)} %fusion.7, f32[139,8,512]{2,1,0:T(8,128)S(1)} %slice.67, f32[1,8,512]{2,1,0:T(8,128)S(1)} %collective-permute-done.3, f32[140,512]{1,0:T(8,128)S(1)} %copy-done.16, ...), kind=kLoop, calls=%fused_computation.22 | loop fusion | flops 10895359 | bytes 17539640 | tf_op jit(solution)/shard_map/reduce_sum | solution.py:87
  186.8 3.9 %all_gather.15 = f32[140,1024]{1,0:T(8,128)} all-gather(f32[140,512]{1,0:T(8,128)} %get-tuple-element.38), channel_id=1, replica_groups=mesh['hour'=16,'region'=2] {'region'}, dimensions={1}, use_global_device_ids=true | all-gather | bytes 860160 | tf_op jit(solution)/shard_map/all_gather | solution.py:111
  190.7 36.8 %psum.31 = f32[]{:T(128)} all-reduce(f32[]{:T(128)S(6)} %add.169), channel_id=1, replica_groups=mesh['hour'=16,'region'=2] {'hour','region'}, use_global_device_ids=true, to_apply=%region_14.0 | all-reduce | flops 1 | bytes 8 | tf_op jit(solution)/shard_map/psum | solution.py:94
  228.2 2.2 add_reduce_fusion
  230.4 75.8 %psum.30 = f32[8,512]{1,0:T(8,128)S(1)} all-reduce(f32[8,512]{1,0:T(8,128)S(1)} %add_reduce_fusion), channel_id=1, replica_groups=mesh['hour'=16,'region'=2] {'hour'}, use_global_device_ids=true, to_apply=%region_9.0 | all-reduce | flops 4096 | bytes 32768 | tf_op jit(solution)/shard_map/psum | solution.py:93
  306.9 5.3 %add_maximum_fusion = (f32[140,8,512]{2,1,0:T(8,128)}, f32[140,8,512]{2,1,0:T(8,128)S(1)}) fusion(f32[140,8,512]{2,1,0:T(8,128)} %get-tuple-element.22, bf16[140,8,512]{2,1,0:T(8,128)(2,1)S(1)} %copy-done.7, f32[8,512]{1,0:T(8,128)S(1)} %get-tuple-element.10, f32[]{:T(128)S(6)} %div.23, f32[140]{0:T(256)} %copy-done.33, ...), kind=kLoop, calls=%fused_computation.20 | loop fusion | flops 5734400 | bytes 12649012 | tf_op jit(solution)/shard_map/max | solution.py:115
  312.2 2.3 fusion.40
  314.9 1.1 collective-permute-done.7
  316.0 2.3 fusion.15
  318.3 1.0 fusion.30
  (106 shorter events, 9.5 us)
Async XLA Ops:
  1.4 20.5 %collective-permute-start.1 = (f32[1,512]{1,0:T(1,128)S(1)}, f32[1,512]{1,0:T(1,128)S(1)}, u32[]{:S(2)}, u32[]{:S(2)}) collective-permute-start(f32[1,512]{1,0:T(1,128)S(1)} %slice.50), channel_id=1, source_target_pairs={{30,0},{0,2},{2,4},{4,6},{6,8},{8,10},{10,12},{12,14},{14,16},{16,... | collective-permute-start | bytes 6152 | tf_op jit(solution)/shard_map/ppermute | solution.py:18
  5.0 25.2 %collective-permute-start = (f32[1,8,512]{2,1,0:T(8,128)S(1)}, f32[1,8,512]{2,1,0:T(8,128)S(1)}, u32[]{:S(2)}, u32[]{:S(2)}) collective-permute-start(f32[1,8,512]{2,1,0:T(8,128)S(1)} %slice.48), channel_id=1, source_target_pairs={{30,0},{0,2},{2,4},{4,6},{6,8},{8,10},{10,12},{12,14},{14,16},{16,... | collective-permute-start | bytes 49160 | tf_op jit(solution)/shard_map/ppermute | solution.py:18
  12.2 152.8 %copy-start = (f32[512,1024]{1,0:T(8,128)}, f32[512,1024]{1,0:T(8,128)S(1)}, u32[]{:S(2)}) copy-start(f32[512,1024]{1,0:T(8,128)S(1)} %bitcast_multiply_fusion) | copy-start | bytes 6291460
  21.1 59.1 %copy-start.33 = (f32[140]{0:T(256)}, f32[140]{0:T(256)S(1)}, u32[]{:S(2)}) copy-start(f32[140]{0:T(256)S(1)} %compare_convert_fusion) | copy-start | bytes 1684
  21.2 9.0 %copy-start.5 = (f32[140,8,512]{2,1,0:T(8,128)S(1)}, f32[140,8,512]{2,1,0:T(8,128)}, u32[]{:S(2)}) copy-start(f32[140,8,512]{2,1,0:T(8,128)} %param.35) | copy-start | bytes 6881284
  21.2 9.0 %copy-start.7 = (bf16[140,8,512]{2,1,0:T(8,128)(2,1)S(1)}, bf16[140,8,512]{2,1,0:T(8,128)(2,1)}, u32[]{:S(2)}) copy-start(bf16[140,8,512]{2,1,0:T(8,128)(2,1)} %param.19) | copy-start | bytes 3440644
  21.9 8.4 %slice-start = ((f32[140,8,512]{2,1,0:T(8,128)}), f32[139,8,512]{2,1,0:T(8,128)S(1)}, s32[]{:S(2)}) async-start(f32[140,8,512]{2,1,0:T(8,128)} %param.35), calls=%async_computation | async-start | bytes 4554752 | tf_op jit(solution)/shard_map/slice | solution.py:73
  21.9 8.4 %copy-start.29 = (f32[8,512]{1,0:T(8,128)S(1)}, f32[8,512]{1,0:T(8,128)}, u32[]{:S(2)}) copy-start(f32[8,512]{1,0:T(8,128)} %param.23) | copy-start | bytes 49156
  21.9 8.4 %copy-start.32 = (f32[8,512]{1,0:T(8,128)S(1)}, f32[8,512]{1,0:T(8,128)}, u32[]{:S(2)}) copy-start(f32[8,512]{1,0:T(8,128)} %param.21) | copy-start | bytes 49156
  25.3 4.8 %copy-start.13 = (f32[140,512]{1,0:T(8,128)}, f32[140,512]{1,0:T(8,128)S(1)}, u32[]{:S(2)}) copy-start(f32[140,512]{1,0:T(8,128)S(1)} %get-tuple-element.24) | copy-start | bytes 860164
  26.1 10.3 %copy-start.8 = (f32[140,8,512]{2,1,0:T(8,128)S(1)}, f32[140,8,512]{2,1,0:T(8,128)}, u32[]{:S(2)}) copy-start(f32[140,8,512]{2,1,0:T(8,128)} %param.27) | copy-start | bytes 6881284
  26.1 54.2 %collective-permute-start.4 = (f32[1,512]{1,0:T(1,128)S(1)}, f32[1,512]{1,0:T(1,128)S(1)}, u32[]{:S(2)}, u32[]{:S(2)}) collective-permute-start(f32[1,512]{1,0:T(1,128)S(1)} %slice.69), channel_id=1, source_target_pairs={{2,0},{4,2},{6,4},{8,6},{10,8},{12,10},{14,12},{16,14},{18,16},{20... | collective-permute-start | bytes 6152 | tf_op jit(solution)/shard_map/ppermute | solution.py:18
  83.6 86.2 %copy-start.30 = (f32[8,512]{1,0:T(8,128)S(1)}, f32[8,512]{1,0:T(8,128)}, u32[]{:S(2)}) copy-start(f32[8,512]{1,0:T(8,128)} %param.31) | copy-start | bytes 49156
  83.6 86.2 %copy-start.31 = (f32[8,512]{1,0:T(8,128)S(1)}, f32[8,512]{1,0:T(8,128)}, u32[]{:S(2)}) copy-start(f32[8,512]{1,0:T(8,128)} %param.22) | copy-start | bytes 49156
  84.3 85.8 %collective-permute-start.5 = (f32[1,512]{1,0:T(1,128)S(1)}, f32[1,512]{1,0:T(1,128)S(1)}, u32[]{:S(2)}, u32[]{:S(2)}) collective-permute-start(f32[1,512]{1,0:T(1,128)S(1)} %slice.70), channel_id=1, source_target_pairs={{30,0},{0,2},{2,4},{4,6},{6,8},{8,10},{10,12},{12,14},{14,16},{16,... | collective-permute-start | bytes 6152 | tf_op jit(solution)/shard_map/ppermute | solution.py:18
  161.5 8.3 %copy-start.4 = (f32[140,8,512]{2,1,0:T(8,128)S(1)}, f32[140,8,512]{2,1,0:T(8,128)}, u32[]{:S(2)}) copy-start(f32[140,8,512]{2,1,0:T(8,128)} %get-tuple-element.26) | copy-start | bytes 6881284
  162.4 9.3 %collective-permute-start.2 = (f32[1,8,512]{2,1,0:T(8,128)S(1)}, f32[1,8,512]{2,1,0:T(8,128)S(1)}, u32[]{:S(2)}, u32[]{:S(2)}) collective-permute-start(f32[1,8,512]{2,1,0:T(8,128)S(1)} %slice.65), channel_id=1, source_target_pairs={{2,0},{4,2},{6,4},{8,6},{10,8},{12,10},{14,12},{16,14},{18,16},{20... | collective-permute-start | bytes 49160 | tf_op jit(solution)/shard_map/ppermute | solution.py:18
  171.7 3.0 copy-start.27
  172.6 7.4 %collective-permute-start.3 = (f32[1,8,512]{2,1,0:T(8,128)S(1)}, f32[1,8,512]{2,1,0:T(8,128)S(1)}, u32[]{:S(2)}, u32[]{:S(2)}) collective-permute-start(f32[1,8,512]{2,1,0:T(8,128)S(1)} %slice.66), channel_id=1, source_target_pairs={{30,0},{0,2},{2,4},{4,6},{6,8},{8,10},{10,12},{12,14},{14,16},{16,... | collective-permute-start | bytes 49160 | tf_op jit(solution)/shard_map/ppermute | solution.py:18
  174.7 5.3 %copy-start.9 = (f32[140,8,512]{2,1,0:T(8,128)S(1)}, f32[140,8,512]{2,1,0:T(8,128)}, u32[]{:S(2)}) copy-start(f32[140,8,512]{2,1,0:T(8,128)} %param.34) | copy-start | bytes 6881284
  175.3 4.7 %copy-start.3 = (f32[140,8,512]{2,1,0:T(8,128)S(1)}, f32[140,8,512]{2,1,0:T(8,128)}, u32[]{:S(2)}) copy-start(f32[140,8,512]{2,1,0:T(8,128)} %copy-done.2) | copy-start | bytes 6881284
  175.3 4.7 %copy-start.16 = (f32[140,512]{1,0:T(8,128)S(1)}, f32[140,512]{1,0:T(8,128)}, u32[]{:S(2)}) copy-start(f32[140,512]{1,0:T(8,128)} %get-tuple-element.19) | copy-start | bytes 860164
  175.3 4.7 %copy-start.34 = (f32[140]{0:T(256)S(1)}, f32[140]{0:T(256)}, u32[]{:S(2)}) copy-start(f32[140]{0:T(256)} %copy-done.33) | copy-start | bytes 1684
  306.9 5.4 %copy-start.1 = (f32[512,1024]{1,0:T(8,128)S(1)}, f32[512,1024]{1,0:T(8,128)}, u32[]{:S(2)}) copy-start(f32[512,1024]{1,0:T(8,128)} %copy-done) | copy-start | bytes 6291460
  306.9 5.4 %copy-start.22 = (f32[140,1024]{1,0:T(8,128)S(1)}, f32[140,1024]{1,0:T(8,128)}, u32[]{:S(2)}) copy-start(f32[140,1024]{1,0:T(8,128)} %all_gather.15) | copy-start | bytes 1720324
  312.2 2.4 copy-start.19
  312.2 3.7 %collective-permute-start.7 = (f32[1,8,512]{2,1,0:T(8,128)S(1)}, f32[1,8,512]{2,1,0:T(8,128)S(1)}, u32[]{:S(2)}, u32[]{:S(2)}) collective-permute-start(f32[1,8,512]{2,1,0:T(8,128)S(1)} %slice.75), channel_id=1, source_target_pairs={{2,0},{4,2},{6,4},{8,6},{10,8},{12,10},{14,12},{16,14},{18,16},{20... | collective-permute-start | bytes 49160 | tf_op jit(solution)/shard_map/ppermute | solution.py:18
  314.6 3.6 %collective-permute-start.6 = (f32[1,512]{1,0:T(1,128)S(1)}, f32[1,512]{1,0:T(1,128)S(1)}, u32[]{:S(2)}, u32[]{:S(2)}) collective-permute-start(f32[1,512]{1,0:T(1,128)S(1)} %slice.73), channel_id=1, source_target_pairs={{2,0},{4,2},{6,4},{8,6},{10,8},{12,10},{14,12},{16,14},{18,16},{20... | collective-permute-start | bytes 6152 | tf_op jit(solution)/shard_map/ppermute | solution.py:18
  315.9 2.3 copy-start.21
  316.0 2.3 copy-start.25
  316.0 2.3 copy-start.26
  316.0 2.3 copy-start.35
  (14 other events, 17.7 us)
where the time goes:
time: 320 us; the launch traced here: 319 us
  blocking collectives  236 us (74%)
  other arithmetic  34 us (11%)
  matrix products  13.8 us (4%)
  starting transfers between devices  13 us (4%)
  local copies, waits for them, and re-layouts  8.49 us (3%)
  between operations  8.08 us (3%)
  waiting for transfers between devices  5.53 us (2%)
    psum x2, blocking collectives, per_device(): invest = lax.psum(invest_part, 'hour')  151 us
    psum x2, blocking collectives, per_device(): squares = lax.psum(square_part, ('hour', 'region'))  74.5 us
    dot_general x4, matrix products, fold_part(): lax.dot_general(segment, matrix, (((1,), (1,)), ((), ())), precision=lax....  13.8 us
    ppermute x8, starting transfers between devices, shifted(): return lax.ppermute(block, axis, route)  13 us
  transfers between devices with their start and end apart: 8, of which 2 were waited for; matrix products, arithmetic and copies ran while one was open for 11% of the time, Pallas kernels for 0%

commit v1 on v0

--- a/solution.py
+++ b/solution.py
@@ -90,7 +90,7 @@
             + jnp.sum((lev_new - levels) ** 2)
         )
         invest_part = jnp.sum(available * limit_dual + ramp_rate[None] * ramp_dual, axis=0)
-        invest = lax.psum(invest_part, "hour")
+        invest = jnp.sum(lax.all_gather(invest_part, "hour"), axis=0)
         squares = lax.psum(square_part, ("hour", "region"))
         cap_new = jnp.maximum(
             0.0, capacity - capacity_step * (inv_cost - invest / float(total_hours))

time: 320 us -> 248 us (0.78)
  blocking collectives: 236 us -> 164 us
    psum x2 -> x0, blocking collectives: 151 us -> none  [per_device(): invest = lax.psum(invest_part, 'hour')]
    all_gather x0 -> x2, blocking collectives: none -> 78.5 us  [per_device(): invest = jnp.sum(lax.all_gather(invest_part, 'hour'), axis=0)]
  transfers between devices with their start and end apart: 8 -> 8, of which waited for: 2 -> 2; matrix products, arithmetic and copies ran while one was open for 11% -> 13% of each run, Pallas kernels for 0% -> 0%
where the time goes in v1:
time: 248 us; the launch traced here: 247 us
  blocking collectives  164 us (66%)
  other arithmetic  33 us (13%)
  starting transfers between devices  15.6 us (6%)
  matrix products  12.9 us (5%)
  between operations  8.24 us (3%)
  local copies, waits for them, and re-layouts  6.81 us (3%)
  waiting for transfers between devices  6.24 us (3%)
    all_gather x2, blocking collectives, per_device(): invest = jnp.sum(lax.all_gather(invest_part, 'hour'), axis=0)  78.5 us
    psum x2, blocking collectives, per_device(): squares = lax.psum(square_part, ('hour', 'region'))  74.5 us
    ppermute x8, starting transfers between devices, shifted(): return lax.ppermute(block, axis, route)  15.6 us
    dot_general x4, matrix products, fold_part(): lax.dot_general(segment, matrix, (((1,), (1,)), ((), ())), precision=lax....  12.9 us
    ppermute x8, waiting for transfers between devices, shifted(): return lax.ppermute(block, axis, route)  6.24 us
    all_gather x2, blocking collectives, per_device(): lax.all_gather(ang_bar, 'region', axis=1, tiled=True)  6.09 us
    reduce_sum x1, other arithmetic, per_device(): jnp.sum(gen_bar, axis=1) + pow_bar  6.08 us
    reduce_sum x2, other arithmetic, per_device(): jnp.sum((gen_new - generation) ** 2) + jnp.sum((ang_new - angles) ** 2)  5.5 us
  transfers between devices with their start and end apart: 8, of which 2 were waited for; matrix products, arithmetic and copies ran while one was open for 13% of the time, Pallas kernels for 0%

profile of v1, /device:TPU:0, one launch (start us, length us, event | category | flops | bytes accessed | tf_op | source)
XLA Modules:
  0.0 246.7 jit_solution(11726881796149759888)
XLA Ops:
  1.4 2.9 %collective-permute-start.1 = (f32[1,512]{1,0:T(1,128)S(1)}, f32[1,512]{1,0:T(1,128)S(1)}, u32[]{:S(2)}, u32[]{:S(2)}) collective-permute-start(f32[1,512]{1,0:T(1,128)S(1)} %slice.50), channel_id=1, source_target_pairs={{30,0},{0,2},{2,4},{4,6},{6,8},{8,10},{10,12},{12,14},{14,16},{16,... | collective-permute-start | bytes 6152 | tf_op jit(solution)/shard_map/ppermute | solution.py:18
  5.0 1.5 collective-permute-start
  7.2 2.4 all_gather.24
  9.6 0.8 dynamic-slice_convert_fusion
  12.2 3.7 %multiply_subtract_fusion.7 = (f32[140,512]{1,0:T(8,128)S(1)}, f32[]{:T(128)}, f32[140,512]{1,0:T(8,128)}) fusion(f32[140,512]{1,0:T(8,128)S(1)} %copy-done.30, f32[512,1024]{1,0:T(8,128)S(1)} %bitcast_multiply_fusion, f32[140,1024]{1,0:T(8,128)S(1)} %all_gather.24), kind=kOutput, calls=%fused_computation.61 | convolution fusion | flops 881305600 | bytes 3530756 | tf_op jit(solution)/shard_map/dot_general | solution.py:63
  15.9 2.2 all_gather.25
  18.1 3.0 %fusion.39 = f32[140,512]{1,0:T(8,128)} fusion(f32[140,1024]{1,0:T(8,128)S(1)} %all_gather.25, f32[512,1024]{1,0:T(8,128)S(1)} %bitcast_multiply_fusion), kind=kOutput, calls=%fused_computation.78 | convolution fusion | flops 880803840 | bytes 2957312 | tf_op jit(solution)/shard_map/dot_general | solution.py:63
  22.3 3.1 %multiply_subtract_fusion.6 = (f32[140,512]{1,0:T(8,128)S(1)}, f32[140,512]{1,0:T(8,128)S(1)}, f32[]{:T(128)}, f32[140,512]{1,0:T(8,128)}) fusion(f32[140,512]{1,0:T(8,128)S(1)} %copy-done.25, f32[140,512]{1,0:T(8,128)S(1)} %copy-done.19, f32[139,512]{1,0:T(8,128)S(1)} %bitcast.26, f32[1,512]{1,0:T(1,128)S(1)} %collective-permute-done.1, ...), kind=kLoop, calls=%fused_computation.59 | loop fusion | flops 931839 | bytes 2293764 | tf_op jit(solution)/shard_map/sub | solution.py:103
  26.1 4.1 %collective-permute-start.4 = (f32[1,512]{1,0:T(1,128)S(1)}, f32[1,512]{1,0:T(1,128)S(1)}, u32[]{:S(2)}, u32[]{:S(2)}) collective-permute-start(f32[1,512]{1,0:T(1,128)S(1)} %slice.69), channel_id=1, source_target_pairs={{2,0},{4,2},{6,4},{8,6},{10,8},{12,10},{14,12},{16,14},{18,16},{20... | collective-permute-start | bytes 6152 | tf_op jit(solution)/shard_map/ppermute | solution.py:18
  30.3 6.1 %fusion.36 = (f32[140,512]{1,0:T(8,128)}, f32[140,8,512]{2,1,0:T(8,128)}, f32[140,8,512]{2,1,0:T(8,128)S(1)}, f32[8,512]{1,0:T(8,128)S(1)}) fusion(f32[140,8,512]{2,1,0:T(8,128)} %param.27, f32[140,8,512]{2,1,0:T(8,128)S(1)} %copy-done.6, f32[139,8,512]{2,1,0:T(8,128)S(1)} %slice-done, f32[1,8,512]{2,1,0:T(8,128)S(1)} %collective-permute-done, ...), kind=kLoop, calls=%fused_computation.76 | loop fusion | flops 10246144 | bytes 15548976 | tf_op jit(solution)/shard_map/reduce_sum | solution.py:109
  36.4 1.3 multiply_reduce_fusion.1
  40.4 1.7 slice.68
  42.1 37.6 %psum.14 = f32[]{:T(128)} all-reduce(f32[]{:T(128)S(6)} %add.145), channel_id=1, replica_groups=mesh['hour'=16,'region'=2] {'hour','region'}, use_global_device_ids=true, to_apply=%region_4.0 | all-reduce | flops 1 | bytes 8 | tf_op jit(solution)/shard_map/psum | solution.py:94
  80.5 3.3 %multiply_reduce_fusion.3 = (f32[]{:T(128)}, f32[140,512]{1,0:T(8,128)}, f32[140,512]{1,0:T(8,128)S(1)}, f32[140,512]{1,0:T(8,128)S(1)}) fusion(f32[140,512]{1,0:T(8,128)} %get-tuple-element.42, f32[140,512]{1,0:T(8,128)} %param.33, f32[140,512]{1,0:T(8,128)} %param.30, f32[140,512]{1,0:T(8,128)} %copy-done.21, f32[1,512]{1,0:T(1,128)S(1)} %collective-permute-done.4, ...), kind=kLoop, calls=%fused_computation.56 | loop fusion | flops 1361919 | bytes 3441208 | tf_op jit(solution)/shard_map/reduce_sum | solution.py:89
  83.8 2.3 collective-permute-start.5
  86.2 3.3 %collective-permute-start.2 = (f32[1,8,512]{2,1,0:T(8,128)S(1)}, f32[1,8,512]{2,1,0:T(8,128)S(1)}, u32[]{:S(2)}, u32[]{:S(2)}) collective-permute-start(f32[1,8,512]{2,1,0:T(8,128)S(1)} %slice.65), channel_id=1, source_target_pairs={{2,0},{4,2},{6,4},{8,6},{10,8},{12,10},{14,12},{16,14},{18,16},{20... | collective-permute-start | bytes 49160 | tf_op jit(solution)/shard_map/ppermute | solution.py:18
  89.5 37.6 %all-gather = f32[128,512]{1,0:T(8,128)S(1)} all-gather(f32[8,512]{1,0:T(8,128)S(1)} %get-tuple-element.32), channel_id=2, replica_groups=mesh['hour'=16,'region'=2] {'hour'}, dimensions={0}, use_global_device_ids=true | all-gather | bytes 278528 | tf_op jit(solution)/shard_map/all_gather | solution.py:93
  127.2 2.4 all_gather.28
  129.6 3.8 %multiply_reduce_fusion.4 = (f32[]{:T(128)}, f32[140,512]{1,0:T(8,128)}, f32[140,512]{1,0:T(8,128)}) fusion(f32[140,512]{1,0:T(8,128)S(1)} %copy-done.29, f32[140,1024]{1,0:T(8,128)S(1)} %all_gather.28, f32[512,1024]{1,0:T(8,128)S(1)} %bitcast_multiply_fusion), kind=kOutput, calls=%fused_computation.57 | convolution fusion | flops 881305600 | bytes 3530756 | tf_op jit(solution)/shard_map/dot_general | solution.py:63
  135.2 0.9 fusion.7
  136.1 1.3 collective-permute-start.3
  138.4 5.2 %collective-permute-done.3 = f32[1,8,512]{2,1,0:T(8,128)S(1)} collective-permute-done((f32[1,8,512]{2,1,0:T(8,128)S(1)}, f32[1,8,512]{2,1,0:T(8,128)S(1)}, u32[]{:S(2)}, u32[]{:S(2)}) %collective-permute-start.3) | collective-permute-done | bytes 16416 | tf_op jit(solution)/shard_map/ppermute | solution.py:18
  143.5 4.2 %multiply_reduce_fusion = (f32[]{:T(128)}, f32[140,8,512]{2,1,0:T(8,128)}, f32[140,8,512]{2,1,0:T(8,128)}) fusion(f32[140,8,512]{2,1,0:T(8,128)S(1)} %copy-done.3, f32[140,8,512]{2,1,0:T(8,128)S(1)} %fusion.7, f32[139,8,512]{2,1,0:T(8,128)S(1)} %slice.67, f32[1,8,512]{2,1,0:T(8,128)S(1)} %collective-permute-done.3, f32[140,512]{1,0:T(8,128)S(1)} %get-tuple-element.19, ...), kind=kLoop, calls=%fused_computation.22 | loop fusion | flops 10895359 | bytes 17539640 | tf_op jit(solution)/shard_map/reduce_sum | solution.py:87
  150.3 3.9 %all_gather.31 = f32[140,1024]{1,0:T(8,128)} all-gather(f32[140,512]{1,0:T(8,128)} %get-tuple-element.38), channel_id=1, replica_groups=mesh['hour'=16,'region'=2] {'region'}, dimensions={1}, use_global_device_ids=true | all-gather | bytes 860160 | tf_op jit(solution)/shard_map/all_gather | solution.py:111
  154.1 36.8 %psum.15 = f32[]{:T(128)} all-reduce(f32[]{:T(128)S(6)} %add.165), channel_id=1, replica_groups=mesh['hour'=16,'region'=2] {'hour','region'}, use_global_device_ids=true, to_apply=%region_14.0 | all-reduce | flops 1 | bytes 8 | tf_op jit(solution)/shard_map/psum | solution.py:94
  191.7 2.3 add_reduce_fusion
  194.0 40.9 %all-gather.1 = f32[128,512]{1,0:T(8,128)S(1)} all-gather(f32[8,512]{1,0:T(8,128)S(1)} %add_reduce_fusion), channel_id=3, replica_groups=mesh['hour'=16,'region'=2] {'hour'}, dimensions={0}, use_global_device_ids=true | all-gather | bytes 278528 | tf_op jit(solution)/shard_map/all_gather | solution.py:93
  235.6 4.0 %add_maximum_fusion = (f32[140,8,512]{2,1,0:T(8,128)}, f32[140,8,512]{2,1,0:T(8,128)S(1)}) fusion(f32[140,8,512]{2,1,0:T(8,128)S(1)} %copy-done.8, bf16[140,8,512]{2,1,0:T(8,128)(2,1)S(1)} %copy-done.9, f32[8,512]{1,0:T(8,128)S(1)} %get-tuple-element.10, f32[]{:T(128)S(6)} %div.23, f32[140]{0:T(256)S(1)} %compare_convert_fusion, ...), kind=kLoop, calls=%fused_computation.20 | loop fusion | flops 5734400 | bytes 12649012 | tf_op jit(solution)/shard_map/max | solution.py:115
  239.7 2.3 fusion.40
  242.3 1.1 collective-permute-done.7
  243.4 2.3 fusion.15
  245.7 1.0 fusion.30
  (106 shorter events, 8.9 us)
Async XLA Ops:
  1.4 20.5 %collective-permute-start.1 = (f32[1,512]{1,0:T(1,128)S(1)}, f32[1,512]{1,0:T(1,128)S(1)}, u32[]{:S(2)}, u32[]{:S(2)}) collective-permute-start(f32[1,512]{1,0:T(1,128)S(1)} %slice.50), channel_id=1, source_target_pairs={{30,0},{0,2},{2,4},{4,6},{6,8},{8,10},{10,12},{12,14},{14,16},{16,... | collective-permute-start | bytes 6152 | tf_op jit(solution)/shard_map/ppermute | solution.py:18
  5.0 25.2 %collective-permute-start = (f32[1,8,512]{2,1,0:T(8,128)S(1)}, f32[1,8,512]{2,1,0:T(8,128)S(1)}, u32[]{:S(2)}, u32[]{:S(2)}) collective-permute-start(f32[1,8,512]{2,1,0:T(8,128)S(1)} %slice.48), channel_id=1, source_target_pairs={{30,0},{0,2},{2,4},{4,6},{6,8},{8,10},{10,12},{12,14},{14,16},{16,... | collective-permute-start | bytes 49160 | tf_op jit(solution)/shard_map/ppermute | solution.py:18
  12.2 117.4 %copy-start = (f32[512,1024]{1,0:T(8,128)}, f32[512,1024]{1,0:T(8,128)S(1)}, u32[]{:S(2)}) copy-start(f32[512,1024]{1,0:T(8,128)S(1)} %bitcast_multiply_fusion) | copy-start | bytes 6291460
  21.2 9.1 %copy-start.6 = (f32[140,8,512]{2,1,0:T(8,128)S(1)}, f32[140,8,512]{2,1,0:T(8,128)}, u32[]{:S(2)}) copy-start(f32[140,8,512]{2,1,0:T(8,128)} %param.35) | copy-start | bytes 6881284
  21.2 9.1 %copy-start.9 = (bf16[140,8,512]{2,1,0:T(8,128)(2,1)S(1)}, bf16[140,8,512]{2,1,0:T(8,128)(2,1)}, u32[]{:S(2)}) copy-start(bf16[140,8,512]{2,1,0:T(8,128)(2,1)} %param.19) | copy-start | bytes 3440644
  21.8 8.4 %slice-start = ((f32[140,8,512]{2,1,0:T(8,128)}), f32[139,8,512]{2,1,0:T(8,128)S(1)}, s32[]{:S(2)}) async-start(f32[140,8,512]{2,1,0:T(8,128)} %param.35), calls=%async_computation | async-start | bytes 4554752 | tf_op jit(solution)/shard_map/slice | solution.py:73
  21.9 8.4 %copy-start.31 = (f32[8,512]{1,0:T(8,128)S(1)}, f32[8,512]{1,0:T(8,128)}, u32[]{:S(2)}) copy-start(f32[8,512]{1,0:T(8,128)} %param.23) | copy-start | bytes 49156
  21.9 8.4 %copy-start.34 = (f32[8,512]{1,0:T(8,128)S(1)}, f32[8,512]{1,0:T(8,128)}, u32[]{:S(2)}) copy-start(f32[8,512]{1,0:T(8,128)} %param.21) | copy-start | bytes 49156
  25.4 4.9 %copy-start.14 = (f32[140,512]{1,0:T(8,128)}, f32[140,512]{1,0:T(8,128)S(1)}, u32[]{:S(2)}) copy-start(f32[140,512]{1,0:T(8,128)S(1)} %get-tuple-element.24) | copy-start | bytes 860164
  26.1 10.3 %copy-start.10 = (f32[140,8,512]{2,1,0:T(8,128)S(1)}, f32[140,8,512]{2,1,0:T(8,128)}, u32[]{:S(2)}) copy-start(f32[140,8,512]{2,1,0:T(8,128)} %param.27) | copy-start | bytes 6881284
  26.1 54.3 %collective-permute-start.4 = (f32[1,512]{1,0:T(1,128)S(1)}, f32[1,512]{1,0:T(1,128)S(1)}, u32[]{:S(2)}, u32[]{:S(2)}) collective-permute-start(f32[1,512]{1,0:T(1,128)S(1)} %slice.69), channel_id=1, source_target_pairs={{2,0},{4,2},{6,4},{8,6},{10,8},{12,10},{14,12},{16,14},{18,16},{20... | collective-permute-start | bytes 6152 | tf_op jit(solution)/shard_map/ppermute | solution.py:18
  80.4 5.7 %copy-start.5 = (f32[140,8,512]{2,1,0:T(8,128)S(1)}, f32[140,8,512]{2,1,0:T(8,128)}, u32[]{:S(2)}) copy-start(f32[140,8,512]{2,1,0:T(8,128)} %get-tuple-element.26) | copy-start | bytes 6881284
  80.5 49.1 %copy-start.29 = (f32[140,512]{1,0:T(8,128)S(1)}, f32[140,512]{1,0:T(8,128)}, u32[]{:S(2)}) copy-start(f32[140,512]{1,0:T(8,128)} %get-tuple-element.43) | copy-start | bytes 860164
  83.8 49.9 %copy-start.12 = (f32[140,512]{1,0:T(8,128)}, f32[140,512]{1,0:T(8,128)S(1)}, u32[]{:S(2)}) copy-start(f32[140,512]{1,0:T(8,128)S(1)} %get-tuple-element.18) | copy-start | bytes 860164
  83.8 59.7 %copy-start.17 = (f32[140,512]{1,0:T(8,128)}, f32[140,512]{1,0:T(8,128)S(1)}, u32[]{:S(2)}) copy-start(f32[140,512]{1,0:T(8,128)S(1)} %get-tuple-element.19) | copy-start | bytes 860164
  83.8 49.8 %collective-permute-start.5 = (f32[1,512]{1,0:T(1,128)S(1)}, f32[1,512]{1,0:T(1,128)S(1)}, u32[]{:S(2)}, u32[]{:S(2)}) collective-permute-start(f32[1,512]{1,0:T(1,128)S(1)} %slice.70), channel_id=1, source_target_pairs={{30,0},{0,2},{2,4},{4,6},{6,8},{8,10},{10,12},{12,14},{14,16},{16,... | collective-permute-start | bytes 6152 | tf_op jit(solution)/shard_map/ppermute | solution.py:18
  86.2 49.1 %collective-permute-start.2 = (f32[1,8,512]{2,1,0:T(8,128)S(1)}, f32[1,8,512]{2,1,0:T(8,128)S(1)}, u32[]{:S(2)}, u32[]{:S(2)}) collective-permute-start(f32[1,8,512]{2,1,0:T(8,128)S(1)} %slice.65), channel_id=1, source_target_pairs={{2,0},{4,2},{6,4},{8,6},{10,8},{12,10},{14,12},{16,14},{18,16},{20... | collective-permute-start | bytes 49160 | tf_op jit(solution)/shard_map/ppermute | solution.py:18
  127.1 6.3 %copy-start.32 = (f32[8,512]{1,0:T(8,128)S(1)}, f32[8,512]{1,0:T(8,128)}, u32[]{:S(2)}) copy-start(f32[8,512]{1,0:T(8,128)} %param.31) | copy-start | bytes 49156
  127.2 6.3 %copy-start.33 = (f32[8,512]{1,0:T(8,128)S(1)}, f32[8,512]{1,0:T(8,128)}, u32[]{:S(2)}) copy-start(f32[8,512]{1,0:T(8,128)} %param.22) | copy-start | bytes 49156
  136.1 7.4 %collective-permute-start.3 = (f32[1,8,512]{2,1,0:T(8,128)S(1)}, f32[1,8,512]{2,1,0:T(8,128)S(1)}, u32[]{:S(2)}, u32[]{:S(2)}) collective-permute-start(f32[1,8,512]{2,1,0:T(8,128)S(1)} %slice.66), channel_id=1, source_target_pairs={{30,0},{0,2},{2,4},{4,6},{6,8},{8,10},{10,12},{12,14},{14,16},{16,... | collective-permute-start | bytes 49160 | tf_op jit(solution)/shard_map/ppermute | solution.py:18
  137.4 6.1 %copy-start.11 = (f32[140,8,512]{2,1,0:T(8,128)S(1)}, f32[140,8,512]{2,1,0:T(8,128)}, u32[]{:S(2)}) copy-start(f32[140,8,512]{2,1,0:T(8,128)} %param.34) | copy-start | bytes 6881284
  138.2 5.4 %copy-start.3 = (f32[140,8,512]{2,1,0:T(8,128)S(1)}, f32[140,8,512]{2,1,0:T(8,128)}, u32[]{:S(2)}) copy-start(f32[140,8,512]{2,1,0:T(8,128)} %copy-done.2) | copy-start | bytes 6881284
  191.7 43.9 %copy-start.4 = (f32[140,8,512]{2,1,0:T(8,128)S(1)}, f32[140,8,512]{2,1,0:T(8,128)}, u32[]{:S(2)}) copy-start(f32[140,8,512]{2,1,0:T(8,128)} %copy-done.2) | copy-start | bytes 6881284
  191.7 43.9 %copy-start.8 = (f32[140,8,512]{2,1,0:T(8,128)S(1)}, f32[140,8,512]{2,1,0:T(8,128)}, u32[]{:S(2)}) copy-start(f32[140,8,512]{2,1,0:T(8,128)} %get-tuple-element.22) | copy-start | bytes 6881284
  235.6 4.0 %copy-start.1 = (f32[512,1024]{1,0:T(8,128)S(1)}, f32[512,1024]{1,0:T(8,128)}, u32[]{:S(2)}) copy-start(f32[512,1024]{1,0:T(8,128)} %copy-done) | copy-start | bytes 6291460
  235.6 4.1 %copy-start.23 = (f32[140,1024]{1,0:T(8,128)S(1)}, f32[140,1024]{1,0:T(8,128)}, u32[]{:S(2)}) copy-start(f32[140,1024]{1,0:T(8,128)} %all_gather.31) | copy-start | bytes 1720324
  239.6 2.4 copy-start.20
  239.6 3.7 %collective-permute-start.7 = (f32[1,8,512]{2,1,0:T(8,128)S(1)}, f32[1,8,512]{2,1,0:T(8,128)S(1)}, u32[]{:S(2)}, u32[]{:S(2)}) collective-permute-start(f32[1,8,512]{2,1,0:T(8,128)S(1)} %slice.75), channel_id=1, source_target_pairs={{2,0},{4,2},{6,4},{8,6},{10,8},{12,10},{14,12},{16,14},{18,16},{20... | collective-permute-start | bytes 49160 | tf_op jit(solution)/shard_map/ppermute | solution.py:18
  242.0 3.6 %collective-permute-start.6 = (f32[1,512]{1,0:T(1,128)S(1)}, f32[1,512]{1,0:T(1,128)S(1)}, u32[]{:S(2)}, u32[]{:S(2)}) collective-permute-start(f32[1,512]{1,0:T(1,128)S(1)} %slice.73), channel_id=1, source_target_pairs={{2,0},{4,2},{6,4},{8,6},{10,8},{12,10},{14,12},{16,14},{18,16},{20... | collective-permute-start | bytes 6152 | tf_op jit(solution)/shard_map/ppermute | solution.py:18
  243.4 2.3 copy-start.22
  243.4 2.3 copy-start.26
  243.4 2.3 copy-start.27
  (13 other events, 18.1 us)
